TPU v7x, 32 devices: a whole 2x2x4 slice. The times are simulated.
32 devices in a mesh: dp: 8 (over z, x), tensor: 4 (over y, core).
Axes of the slice: x: 2, y: 2, z: 4, core: 2. Of those that a mesh axis runs over, the one named last changes fastest.
Arguments:
- patches: bfloat16 [24, 2048, 1024], P('dp', 'tensor'), may hold values from -6 to 6
- cotangent: bfloat16 [24, 2048, 1024], P('dp', 'tensor'), may hold values from -6 to 6
- empty_slots: int32 [8], replicated, may hold values from 0 to 2
- dataset_id: int32 [24], replicated, may hold values from 0 to 5
- dataset_weight: int32 [6], replicated, may hold values from 1 to 8
- query_key_value_weight: bfloat16 [3, 1024, 1024], P(None, None, 'tensor'), may hold values from -0.25 to 0.25
- qv_bias: float32 [2, 1024], P(None, 'tensor'), may hold values from -3 to 3
- output_projection_weight: bfloat16 [1024, 1024], P('tensor'), may hold values from -0.75 to 0.75
- out_bias: float32 [1024], replicated, may hold values from -2 to 2
- up_projection_weight: bfloat16 [1024, 4096], P(None, 'tensor'), may hold values from -0.1875 to 0.1875
- up_bias: float32 [4096], P('tensor'), may hold values from -2 to 2
- down_projection_weight: bfloat16 [4096, 1024], P('tensor'), may hold values from -0.09375 to 0.09375
- down_bias: float32 [1024], replicated, may hold values from -2 to 2
- attn_gain: float32 [1024], replicated, may hold values from 0.5 to 1.5
- attn_shift: float32 [1024], replicated, may hold values from -1.5 to 1.5
- mlp_gain: float32 [1024], replicated, may hold values from 0.5 to 1.5
- mlp_shift: float32 [1024], replicated, may hold values from -1.5 to 1.5
Outputs:
- block_out: bfloat16 [24, 2048, 1024], P('dp', 'tensor')
- grad_patches: bfloat16 [24, 2048, 1024], P('dp', 'tensor')
- grad_qkv_weight: float32 [3, 1024, 1024], P(None, None, 'tensor')
- grad_qv_bias: float32 [2, 1024], P(None, 'tensor')
- grad_out_weight: float32 [1024, 1024], P('tensor')
- grad_out_bias: float32 [1024], replicated
- grad_up_weight: float32 [1024, 4096], P(None, 'tensor')
- grad_up_bias: float32 [4096], P('tensor')
- grad_down_weight: float32 [4096, 1024], P('tensor')
- grad_down_bias: float32 [1024], replicated
- grad_attn_gain: float32 [1024], replicated
- grad_attn_shift: float32 [1024], replicated
- sensitivity_feedforward_scale: float32 [1024], replicated
- grad_mlp_shift: float32 [1024], replicated
All inputs are finite; a program needn't handle non-finite values.
Results may differ from a plain program's by a relative error of at most 0.02.
Values may be sent and summed in bfloat16 or wider, within the bound.
No kernel may reach another device: no remote copies, remote signals or barrier semaphores. Data moves between devices by JAX's collectives and lax.ppermute only.
A program may use at most 256 MiB of HBM per device.

v0:
```python
import jax
import jax.numpy as jnp
from jax import lax
from jax.sharding import PartitionSpec as P

HD = 64
epsilon = 1e-05


def norm_rows(source, norm_gain, norm_shift):
    row_mean = jnp.mean(source, axis=-1, keepdims=True)
    centred = source - row_mean
    spread = jnp.mean(centred * centred, axis=-1, keepdims=True)
    return centred * lax.rsqrt(spread + epsilon) * norm_gain + norm_shift


def gelu_exact(pre_act):
    return jax.nn.gelu(pre_act, approximate=False)


def split_heads(array, head_count):
    return array.reshape(array.shape[0], array.shape[1], head_count, HD)


def attend_item(operands):
    queries, key_rows, values = operands
    length, head_count, head_size = queries.shape
    qblock = min(512, length)
    score_scale = head_size ** (-0.5)
    blocks = queries.reshape(length // qblock, qblock, head_count, head_size)

    def one_block(query_block):
        scores = (
            jnp.einsum("qhd,khd->hqk", query_block, key_rows, preferred_element_type=jnp.float32)
            * score_scale
        )
        row_top = jnp.max(scores, axis=-1, keepdims=True)
        exp_scores = jnp.exp(scores - row_top)
        row_total = jnp.sum(exp_scores, axis=-1, keepdims=True)
        attn_weights = (exp_scores / row_total).astype(jnp.bfloat16)
        attended = jnp.einsum(
            "hqk,khd->qhd", attn_weights, values, preferred_element_type=jnp.float32
        )
        return (attended.astype(jnp.bfloat16), (row_top + jnp.log(row_total))[:, :, 0])

    attended, log_total = lax.map(one_block, blocks)
    return (attended.reshape(length, head_count, head_size), log_total)


def attend_back(operands):
    queries, key_rows, values, grad_attended, log_total = operands
    length, head_count, head_size = queries.shape
    qblock = min(512, length)
    score_scale = head_size ** (-0.5)
    query_blocks = queries.reshape(length // qblock, qblock, head_count, head_size)
    grad_blocks = grad_attended.reshape(length // qblock, qblock, head_count, head_size)

    def one_block(carried, block_in):
        query_block, grad_block, lse_block = block_in
        scores = (
            jnp.einsum("qhd,khd->hqk", query_block, key_rows, preferred_element_type=jnp.float32)
            * score_scale
        )
        attn_weights = jnp.exp(scores - lse_block[:, :, None])
        grad_weights = jnp.einsum(
            "qhd,khd->hqk", grad_block, values, preferred_element_type=jnp.float32
        )
        grad_scores = attn_weights * (
            grad_weights - jnp.sum(attn_weights * grad_weights, axis=-1, keepdims=True)
        )
        grad_low = grad_scores.astype(jnp.bfloat16)
        sensitivity_questions = (
            jnp.einsum("hqk,khd->qhd", grad_low, key_rows, preferred_element_type=jnp.float32)
            * score_scale
        )
        key_acc = (
            carried[0]
            + jnp.einsum("hqk,qhd->khd", grad_low, query_block, preferred_element_type=jnp.float32)
            * score_scale
        )
        value_acc = carried[1] + jnp.einsum(
            "hqk,qhd->khd",
            attn_weights.astype(jnp.bfloat16),
            grad_block,
            preferred_element_type=jnp.float32,
        )
        return ((key_acc, value_acc), sensitivity_questions)

    zero_acc = jnp.zeros((length, head_count, head_size), jnp.float32)
    (grad_keys, grad_values), grad_queries = lax.scan(
        one_block, (zero_acc, zero_acc), (query_blocks, grad_blocks, log_total)
    )
    return (grad_queries.reshape(length, head_count, head_size), grad_keys, grad_values)


def shards(
    patches,
    cotangent,
    empty_slots,
    dataset_id,
    dataset_weight,
    query_key_value_weight,
    qv_bias,
    output_projection_weight,
    out_bias,
    up_projection_weight,
    up_bias,
    down_projection_weight,
    down_bias,
    attn_gain,
    attn_shift,
    mlp_gain,
    mlp_shift,
):
    number_format = jnp.float32
    half_type = jnp.bfloat16
    slot_count = patches.shape[0]
    group_slots = empty_slots.shape[0]
    slot_index = jnp.arange(group_slots * slot_count, dtype=jnp.int32) % slot_count
    filled = jnp.repeat(slot_count - empty_slots, slot_count)
    valid_all = (slot_index < filled).astype(number_format)
    table_hits = (
        dataset_id[:, None] == jnp.arange(dataset_weight.shape[0], dtype=jnp.int32)[None, :]
    )
    numerator = jnp.sum(jnp.where(table_hits, dataset_weight[None, :], 0), axis=1).astype(
        number_format
    )
    total_items = jnp.sum(valid_all)
    total_weight = jnp.sum(valid_all * numerator)
    multiplier_whole = valid_all * numerator * total_items / total_weight
    own_start = lax.axis_index("dp") * slot_count
    own_scale = lax.dynamic_slice_in_dim(multiplier_whole, own_start, slot_count)
    own_valid = lax.dynamic_slice_in_dim(valid_all, own_start, slot_count)
    inputs = patches.astype(number_format)
    normed = norm_rows(inputs, attn_gain, attn_shift).astype(half_type)
    normalized_every = lax.all_gather(normed, "tensor", axis=1, tiled=True)
    local_width = query_key_value_weight.shape[2]
    head_count = local_width // HD
    projected_rows = jnp.einsum(
        "owz,gzh->gowh",
        normalized_every,
        query_key_value_weight,
        preferred_element_type=number_format,
    )
    queries = split_heads((projected_rows[0] + qv_bias[0]).astype(half_type), head_count)
    key_rows = split_heads(projected_rows[1].astype(half_type), head_count)
    values = split_heads((projected_rows[2] + qv_bias[1]).astype(half_type), head_count)
    attended, log_total = lax.map(attend_item, (queries, key_rows, values))
    attended_matrix = attended.reshape(slot_count, attended.shape[1], local_width)
    attn_part = jnp.einsum(
        "ifz,zp->ifp",
        attended_matrix,
        output_projection_weight,
        preferred_element_type=number_format,
    )
    attn_rows = lax.psum_scatter(
        attn_part.astype(jnp.bfloat16), "tensor", scatter_dimension=1, tiled=True
    ).astype(jnp.float32)
    residual = inputs + attn_rows + out_bias
    normed_mlp = norm_rows(residual, mlp_gain, mlp_shift).astype(half_type)
    cot_scaled = cotangent.astype(number_format) * own_scale[:, None, None]
    cot_low = cot_scaled.astype(half_type)
    normalized_perceptron_every = lax.all_gather(normed_mlp, "tensor", axis=1, tiled=True)
    hidden_pre = (
        jnp.einsum(
            "jzb,bu->jzu",
            normalized_perceptron_every,
            up_projection_weight,
            preferred_element_type=number_format,
        )
        + up_bias
    )
    gelu_out, gelu_back = jax.vjp(gelu_exact, hidden_pre)
    latent_activations = gelu_out.astype(half_type)
    perceptron_portion = jnp.einsum(
        "vuc,cy->vuy",
        latent_activations,
        down_projection_weight,
        preferred_element_type=number_format,
    )
    mlp_rows = lax.psum_scatter(
        perceptron_portion.astype(jnp.bfloat16), "tensor", scatter_dimension=1, tiled=True
    ).astype(jnp.float32)
    output = ((residual + mlp_rows + down_bias) * own_valid[:, None, None]).astype(half_type)
    adjoint_for_each_layer = lax.all_gather(cot_low, "tensor", axis=1, tiled=True)
    hidden_gradient = jnp.einsum(
        "eph,wh->epw",
        adjoint_for_each_layer,
        down_projection_weight,
        preferred_element_type=number_format,
    )
    preactivation_gradient = gelu_back(hidden_gradient)[0].astype(half_type)
    down_gradient = jnp.einsum(
        "wuf,wul->fl",
        latent_activations,
        adjoint_for_each_layer,
        preferred_element_type=number_format,
    )
    up_gradient = jnp.einsum(
        "eug,eut->gt",
        normalized_perceptron_every,
        preactivation_gradient,
        preferred_element_type=number_format,
    )
    grad_up_bias = jnp.sum(preactivation_gradient.astype(number_format), axis=(0, 1))
    norm_portion = jnp.einsum(
        "jmn,hn->jmh",
        preactivation_gradient,
        up_projection_weight,
        preferred_element_type=number_format,
    )
    grad_normed_mlp = lax.psum_scatter(
        norm_portion.astype(jnp.bfloat16), "tensor", scatter_dimension=1, tiled=True
    ).astype(jnp.float32)
    mlp_norm_back = jax.vjp(norm_rows, residual, mlp_gain, mlp_shift)[1]
    grad_resid_norm, sensitivity_feedforward_scale, grad_mlp_shift = mlp_norm_back(grad_normed_mlp)
    grad_residual = cot_scaled + grad_resid_norm
    grad_out_bias = jnp.sum(grad_residual, axis=(0, 1))
    grad_down_bias = jnp.sum(cot_scaled, axis=(0, 1))
    residual_gradient_every = lax.all_gather(
        grad_residual.astype(half_type), "tensor", axis=1, tiled=True
    )
    grad_attended = jnp.einsum(
        "xmn,wn->xmw",
        residual_gradient_every,
        output_projection_weight,
        preferred_element_type=number_format,
    ).astype(half_type)
    grad_out = jnp.einsum(
        "ift,ifr->tr",
        attended_matrix,
        residual_gradient_every,
        preferred_element_type=number_format,
    )
    grad_queries, grad_keys, grad_values = lax.map(
        attend_back, (queries, key_rows, values, split_heads(grad_attended, head_count), log_total)
    )
    flat_shape = (slot_count, grad_queries.shape[1], local_width)
    projection_gradient = jnp.stack(
        [
            grad_queries.reshape(flat_shape).astype(half_type),
            grad_keys.reshape(flat_shape).astype(half_type),
            grad_values.reshape(flat_shape).astype(half_type),
        ]
    )
    query_key_value_gradient = jnp.einsum(
        "ktr,jktq->jrq", normalized_every, projection_gradient, preferred_element_type=number_format
    )
    grad_qv = jnp.stack(
        [
            jnp.sum(projection_gradient[0].astype(number_format), axis=(0, 1)),
            jnp.sum(projection_gradient[2].astype(number_format), axis=(0, 1)),
        ]
    )
    normed_part = jnp.einsum(
        "vbmk,vxk->bmx",
        projection_gradient,
        query_key_value_weight,
        preferred_element_type=number_format,
    )
    grad_normed = lax.psum_scatter(
        normed_part.astype(jnp.bfloat16), "tensor", scatter_dimension=1, tiled=True
    ).astype(jnp.float32)
    attn_norm_back = jax.vjp(norm_rows, inputs, attn_gain, attn_shift)[1]
    grad_input_norm, grad_attn_gain, grad_attn_shift = attn_norm_back(grad_normed)
    grad_inputs = (grad_residual + grad_input_norm).astype(half_type)
    summed = (
        lax.psum(query_key_value_gradient.astype(jnp.bfloat16), "dp").astype(jnp.float32),
        lax.psum(grad_qv.astype(jnp.bfloat16), "dp").astype(jnp.float32),
        lax.psum(grad_out.astype(jnp.bfloat16), "dp").astype(jnp.float32),
        lax.psum(up_gradient.astype(jnp.bfloat16), "dp").astype(jnp.float32),
        lax.psum(grad_up_bias.astype(jnp.bfloat16), "dp").astype(jnp.float32),
        lax.psum(down_gradient.astype(jnp.bfloat16), "dp").astype(jnp.float32),
    )
    small_sums = lax.psum(
        (
            grad_attn_gain,
            grad_attn_shift,
            sensitivity_feedforward_scale,
            grad_mlp_shift,
            grad_out_bias,
            grad_down_bias,
        ),
        ("dp", "tensor"),
    )
    return (
        output,
        grad_inputs,
        summed[0] / total_items,
        summed[1] / total_items,
        summed[2] / total_items,
        small_sums[4] / total_items,
        summed[3] / total_items,
        summed[4] / total_items,
        summed[5] / total_items,
        small_sums[5] / total_items,
        small_sums[0] / total_items,
        small_sums[1] / total_items,
        small_sums[2] / total_items,
        small_sums[3] / total_items,
    )


def solution(mesh):
    placed = (
        P("dp", "tensor", None),
        P("dp", "tensor", None),
        P(),
        P(),
        P(),
        P(None, None, "tensor"),
        P(None, "tensor"),
        P("tensor", None),
        P(),
        P(None, "tensor"),
        P("tensor"),
        P("tensor", None),
        P(),
        P(),
        P(),
        P(),
        P(),
    )
    return jax.shard_map(
        shards,
        mesh=mesh,
        in_specs=placed,
        out_specs=(
            P("dp", "tensor", None),
            P("dp", "tensor", None),
            P(None, None, "tensor"),
            P(None, "tensor"),
            P("tensor", None),
            P(),
            P(None, "tensor"),
            P("tensor"),
            P("tensor", None),
            P(),
            P(),
            P(),
            P(),
            P(),
        ),
        check_vma=False,
    )
```

profile of v0, /device:TPU:0, one launch (start us, length us, event | category | flops | bytes accessed | tf_op | source)
XLA Modules:
  0.0 1974.1 jit_solution(18060391247935320922)
XLA Ops:
  16.7 84.7 %all-gather.5.cloned.1.call-done = bf16[3,2048,1024]{2,1,0:T(8,128)(2,1)} async-done(((bf16[3,512,1024]{2,1,0:T(8,128)(2,1)}), bf16[3,2048,1024]{2,1,0:T(8,128)(2,1)}) %all-gather.5.cloned.1.call-update) | async-done | bytes 12582928 | tf_op jit(solution)/shard_map/all_gather | solution.py:136
  101.4 17.1 fusion.58
  123.4 11.4 fusion.102
  144.1 192.9 %while.54 = (s32[]{:T(128)}, bf16[3,2048,4,64]{1,3,2,0:T(8,128)(2,1)}, f32[3,4,4,512]{3,2,1,0:T(4,128)}, bf16[3,2048,4,64]{1,3,2,0:T(8,128)(2,1)}, bf16[3,2048,4...) while((s32[]{:T(128)}, ...), condition=%wide.region_7.8_spmd, body=%wide.region_2.7_spmd.sunk | while | flops 1111619584 | bytes 74055984 | solution.py:148
  152.4 47.4 %while.57 = (s32[]{:T(128)}, bf16[4,512,4,64]{1,3,2,0:T(8,128)(2,1)}, f32[4,4,512]{2,1,0:T(4,128)S(1)}, bf16[4,512,4,64]{1,3,2,0:T(8,128)(2,1)}, bf16[2048,4,64]...) while((s32[]{:T(128)}, bf16[4,512,4,64]{1,3,2,0:T(8,128)(2,1)}, ...), condition=%wide.region_6.6_spmd, body=%wide.region_3.5_spmd.sunk | while | flops 1111619584 | bytes 57213052 | solution.py:46
  216.6 47.4 %while.57 = (s32[]{:T(128)}, bf16[4,512,4,64]{1,3,2,0:T(8,128)(2,1)}, f32[4,4,512]{2,1,0:T(4,128)S(1)}, bf16[4,512,4,64]{1,3,2,0:T(8,128)(2,1)}, bf16[2048,4,64]...) while((s32[]{:T(128)}, bf16[4,512,4,64]{1,3,2,0:T(8,128)(2,1)}, ...), condition=%wide.region_6.6_spmd, body=%wide.region_3.5_spmd.sunk | while | flops 1111619584 | bytes 57213052 | solution.py:46
  280.8 47.4 %while.57 = (s32[]{:T(128)}, bf16[4,512,4,64]{1,3,2,0:T(8,128)(2,1)}, f32[4,4,512]{2,1,0:T(4,128)S(1)}, bf16[4,512,4,64]{1,3,2,0:T(8,128)(2,1)}, bf16[2048,4,64]...) while((s32[]{:T(128)}, bf16[4,512,4,64]{1,3,2,0:T(8,128)(2,1)}, ...), condition=%wide.region_6.6_spmd, body=%wide.region_3.5_spmd.sunk | while | flops 1111619584 | bytes 57213052 | solution.py:46
  347.1 99.1 %reduce-scatter.5.cloned.1.call-done = bf16[3,512,1024]{2,1,0:T(8,128)(2,1)} async-done(((bf16[3,2048,1024]{2,1,0:T(8,128)(2,1)}), bf16[3,512,1024]{2,1,0:T(8,128)(2,1)}) %reduce-scatter.5.cloned.1.call-update) | async-done | bytes 3145744 | tf_op jit(solution)/shard_map/reduce_scatter | solution.py:156
  465.1 73.9 %all-gather.7.cloned.1.call-done = bf16[3,2048,1024]{2,1,0:T(8,128)(2,1)} async-done(((bf16[3,512,1024]{2,1,0:T(8,128)(2,1)}), bf16[3,2048,1024]{2,1,0:T(8,128)(2,1)}) %all-gather.7.cloned.1.call-update) | async-done | bytes 12582928 | tf_op jit(solution)/shard_map/all_gather | solution.py:163
  539.1 29.6 %fusion.72 = (u8[2048,1024]{1,0:T(8,128)(4,1)}, u8[2048,1024]{1,0:T(8,128)(4,1)}, f32[3,2048,1024]{2,1,0:T(8,128)}) fusion(f32[1024]{0:T(1024)S(1)} %copy-done.41, bf16[3,2048,1024]{2,1,0:T(8,128)(2,1)} %all-gather.7.cloned.1.call-done, bf16[1024,1024]{1,0:T(8,128)(2,1)S(1)} %copy-done), kind=kOutput, calls=%fused_computation.128 | convolution fusion | flops 12968787968 | bytes 44044288 | tf_op jit(solution)/shard_map/jzb,bu->jzu/dot_general | solution.py:165
  568.7 61.6 %multiply_convert_fusion.1 = (bf16[3,2048,1024]{2,1,0:T(8,128)(2,1)}, f32[3,2048,1024]{2,1,0:T(8,128)}) fusion(f32[3,2048,1024]{2,1,0:T(8,128)} %get-tuple-element.412, f32[1024]{0:T(1024)S(1)} %copy-done.41, u8[2048,1024]{1,0:T(8,128)(4,1)} %get-tuple-element.313, u8[2048,1024]{1,0:T(8,128)(4,1)} %get-tuple-element.312), kind=kLoop, calls=%fused_computation.67 | loop fusion | flops 446693376 | bytes 67112960 | tf_op jit(solution)/shard_map/convert_element_type | solution.py:174
  630.3 32.6 %fusion.103 = (bf16[1024]{0:T(1024)(128)(2,1)}, bf16[3,2048,1024]{2,1,0:T(8,128)(2,1)}) fusion(f32[3,2048,1024]{2,1,0:T(8,128)} %get-tuple-element.399, bf16[3,2048,1024]{2,1,0:T(8,128)(2,1)} %all-gather.9.cloned.1.call-done, bf16[1024,1024]{1,0:T(8,128)(2,1)} %param.36, f32[3,2048,1024]{2,1,0:T(8,128)} %get-tuple-element.412, f32[1024]{0:T(1024)S(1)} %copy-done.41), kind=kOutput, calls=%fused_computation.192 | convolution fusion | flops 12985564160 | bytes 77600768 | tf_op jit(solution)/shard_map/eph,wh->epw/dot_general | solution.py:186
  662.9 20.4 %convolution_convert_fusion = bf16[3,2048,1024]{2,1,0:T(8,128)(2,1)} fusion(bf16[3,2048,1024]{2,1,0:T(8,128)(2,1)} %get-tuple-element.414, bf16[1024,1024]{1,0:T(8,128)(2,1)S(1)} %copy-done), kind=kOutput, calls=%fused_computation.105 | convolution fusion | flops 12891193344 | bytes 27262976 | tf_op jit(solution)/shard_map/jmn,hn->jmh/dot_general | solution.py:206
  684.8 21.3 %convolution_convert_fusion.1 = bf16[3,2048,1024]{2,1,0:T(8,128)(2,1)} fusion(bf16[3,2048,1024]{2,1,0:T(8,128)(2,1)} %get-tuple-element.398, bf16[1024,1024]{1,0:T(8,128)(2,1)S(1)} %copy-done.47), kind=kOutput, calls=%fused_computation.106 | convolution fusion | flops 12891193344 | bytes 27262976 | tf_op jit(solution)/shard_map/vuc,cy->vuy/dot_general | solution.py:175
  706.3 76.2 %reduce-scatter.9.cloned.1.call-done = bf16[3,512,1024]{2,1,0:T(8,128)(2,1)} async-done(((bf16[3,2048,1024]{2,1,0:T(8,128)(2,1)}), bf16[3,512,1024]{2,1,0:T(8,128)(2,1)}) %reduce-scatter.9.cloned.1.call-update) | async-done | bytes 3145744 | tf_op jit(solution)/shard_map/reduce_scatter | solution.py:212
  795.7 88.3 %reduce-scatter.7.cloned.1.call-done = bf16[3,512,1024]{2,1,0:T(8,128)(2,1)} async-done(((bf16[3,2048,1024]{2,1,0:T(8,128)(2,1)}), bf16[3,512,1024]{2,1,0:T(8,128)(2,1)}) %reduce-scatter.7.cloned.1.call-update) | async-done | bytes 3145744 | tf_op jit(solution)/shard_map/reduce_scatter | solution.py:181
  899.3 19.5 bitcast_convert_fusion.1
  918.9 19.0 bitcast_convert_fusion.2
  937.8 43.7 %all-gather.11.cloned.1.call-done = bf16[3,2048,1024]{2,1,0:T(8,128)(2,1)} async-done(((bf16[3,512,1024]{2,1,0:T(8,128)(2,1)}), bf16[3,2048,1024]{2,1,0:T(8,128)(2,1)}) %all-gather.11.cloned.1.call-update) | async-done | bytes 12582928 | tf_op jit(solution)/shard_map/all_gather | solution.py:220
  981.5 14.3 convolution_convert_fusion.3
  995.9 553.7 %while.56 = (s32[]{:T(128)}, bf16[3,2048,4,64]{1,3,2,0:T(8,128)(2,1)}, bf16[3,2048,4,64]{1,3,2,0:T(8,128)(2,1)}, bf16[3,2048,4,64]{1,3,2,0:T(8,128)(2,1)}, bf16[...) while((s32[]{:T(128)}, ...), condition=%wide.region_22.23_spmd, body=%wide.region_18.22_spmd.sunk | while | flops 2737436672 | bytes 246014544 | solution.py:235
  1010.8 158.2 %while.58 = (s32[]{:T(128)}, f32[2048,4,64]{0,2,1:T(8,128)}, f32[2048,4,64]{0,2,1:T(8,128)}, bf16[4,512,4,64]{1,3,2,0:T(8,128)(2,1)}, bf16[4,512,4,64]{1,3,2,0:T...) while((s32[]{:T(128)}, f32[2048,4,64]{0,2,1:T(8,128)}, ...), condition=%wide.region_21.21_spmd.clone, body=%wide.region_19.20_spmd.clone.sunk | while | flops 2737436672 | bytes 206102832 | solution.py:90
  1028.9 10.6 multiply_convert_fusion.4
  1068.4 10.6 multiply_convert_fusion.4
  1195.3 158.2 %while.58 = (s32[]{:T(128)}, f32[2048,4,64]{0,2,1:T(8,128)}, f32[2048,4,64]{0,2,1:T(8,128)}, bf16[4,512,4,64]{1,3,2,0:T(8,128)(2,1)}, bf16[4,512,4,64]{1,3,2,0:T...) while((s32[]{:T(128)}, f32[2048,4,64]{0,2,1:T(8,128)}, ...), condition=%wide.region_21.21_spmd.clone, body=%wide.region_19.20_spmd.clone.sunk | while | flops 2737436672 | bytes 206102832 | solution.py:90
  1379.8 158.2 %while.58 = (s32[]{:T(128)}, f32[2048,4,64]{0,2,1:T(8,128)}, f32[2048,4,64]{0,2,1:T(8,128)}, bf16[4,512,4,64]{1,3,2,0:T(8,128)(2,1)}, bf16[4,512,4,64]{1,3,2,0:T...) while((s32[]{:T(128)}, f32[2048,4,64]{0,2,1:T(8,128)}, ...), condition=%wide.region_21.21_spmd.clone, body=%wide.region_19.20_spmd.clone.sunk | while | flops 2737436672 | bytes 206102832 | solution.py:90
  1573.3 13.9 fusion.86
  1588.6 15.4 bitcast_convert_fusion
  1609.1 22.8 %all-reduce.1 = (bf16[2,256]{1,0:T(2,128)(2,1)S(1)}, bf16[1024]{0:T(1024)(128)(2,1)S(1)}) all-reduce(bf16[2,256]{1,0:T(2,128)(2,1)S(1)} %pad_maximum_fusion.7, bf16[1024]{0:T(1024)(128)(2,1)S(1)} %copy-done.45), channel_id=1, replica_groups=mesh['dp'=8,'tensor'=4] {'dp'}, use_global_device_ids=true, to_apply=%region_29.30 | all-reduce | flops 1536 | bytes 6144 | tf_op jit(solution)/shard_map/psum | solution.py:269
  1634.4 167.8 %all-reduce.5.cloned.1.call-done = (bf16[3,1024,256]{1,2,0:T(8,128)(2,1)}, bf16[256,1024]{1,0:T(8,128)(2,1)}, bf16[1024,1024]{1,0:T(8,128)(2,1)}, bf16[1024,1024]{1,0:T(8,128)(2,1)}) async-done(((bf16[3,1024,256]{1,2,0:T(8,128)(2,1)}, bf16[256,1024]{1,0:T(8,128)(2,1)}, bf16[1024,1024]{1,0:T(8,128)(2,1)}, bf16[1024,1024]{1,0:T(8,128)(2,1)}), (bf16[3,1024,256]{1,2,0:T(8,128)(2,1)}, ...) | async-done | bytes 6291472 | tf_op jit(solution)/shard_map/psum | solution.py:268
  1821.7 81.2 %reduce-scatter.11.cloned.1.call-done = bf16[3,512,1024]{2,1,0:T(8,128)(2,1)} async-done(((bf16[3,2048,1024]{2,1,0:T(8,128)(2,1)}), bf16[3,512,1024]{2,1,0:T(8,128)(2,1)}) %reduce-scatter.11.cloned.1.call-update) | async-done | bytes 3145744 | tf_op jit(solution)/shard_map/reduce_scatter | solution.py:261
  1912.9 39.7 %all-reduce = (f32[1024]{0:T(1024)S(1)}, f32[1024]{0:T(1024)S(1)}, f32[1024]{0:T(1024)S(1)}, f32[1024]{0:T(1024)S(1)}, f32[1024]{0:T(1024)S(1)}, /*index=5*/f32[1024]{0:T(1024)S(1)}) all-reduce(f32[1024]{0:T(1024)S(1)} %copy-done.37, f32[1024]{0:T(1024)S(1)} %copy-done.38, ...), channel_id=1, replica_groups=mesh['dp'=8,'tensor'=4] {'dp','tensor'}, use_global_device_ids=true, to_apply=%region_32.33 | all-reduce | flops 6144 | bytes 49152 | tf_op jit(solution)/shard_map/psum | solution.py:275
  (534 shorter events, 883.0 us)
Async XLA Ops:
  7.2 531.9 %copy-start = (bf16[1024,1024]{1,0:T(8,128)(2,1)S(1)}, bf16[1024,1024]{1,0:T(8,128)(2,1)}, u32[]{:S(2)}) copy-start(bf16[1024,1024]{1,0:T(8,128)(2,1)} %param.34) | copy-start | bytes 6291460
  7.2 94.1 %all-gather.5.cloned.1.call-start = ((), (), s32[]{:S(2)}) async-start(), calls=%async_computation.4 | async-start | bytes 15728640 | tf_op jit(solution)/shard_map/all_gather | solution.py:136
  16.4 429.9 %reduce-scatter.5.cloned.1.call-start = ((), (), s32[]{:S(2)}) async-start(), calls=%async_computation.5 | async-start | bytes 15728640 | tf_op jit(solution)/shard_map/reduce_scatter | solution.py:156
  347.0 99.2 %copy-start.23 = (f32[1024]{0:T(1024)S(1)}, f32[1024]{0:T(1024)}, u32[]{:S(2)}) copy-start(f32[1024]{0:T(1024)} %param.33) | copy-start | bytes 12292
  347.1 106.7 %copy-start.32 = (f32[1024]{0:T(1024)S(1)}, f32[1024]{0:T(1024)}, u32[]{:S(2)}) copy-start(f32[1024]{0:T(1024)} %param.40) | copy-start | bytes 12292
  347.1 106.7 %copy-start.39 = (f32[1024]{0:T(1024)S(1)}, f32[1024]{0:T(1024)}, u32[]{:S(2)}) copy-start(f32[1024]{0:T(1024)} %param.41) | copy-start | bytes 12292
  347.1 192.0 %all-gather.7.cloned.1.call-start = ((), (), s32[]{:S(2)}) async-start(), calls=%async_computation.6 | async-start | bytes 15728640 | tf_op jit(solution)/shard_map/all_gather | solution.py:163
  456.8 82.3 %copy-start.41 = (f32[1024]{0:T(1024)S(1)}, f32[1024]{0:T(1024)}, u32[]{:S(2)}) copy-start(f32[1024]{0:T(1024)} %param.35) | copy-start | bytes 12292
  456.8 173.5 %all-gather.9.cloned.1.call-start = ((), (), s32[]{:S(2)}) async-start(), calls=%async_computation.8 | async-start | bytes 15728640 | tf_op jit(solution)/shard_map/all_gather | solution.py:185
  460.3 108.4 %copy-start.43 = (f32[3]{0:T(128)}, f32[3]{0:T(128)S(1)}, u32[]{:S(2)}) copy-start(f32[3]{0:T(128)S(1)} %dynamic_slice.47) | copy-start | bytes 40
  465.1 317.4 %reduce-scatter.9.cloned.1.call-start = ((), (), s32[]{:S(2)}) async-start(), calls=%async_computation.9 | async-start | bytes 15728640 | tf_op jit(solution)/shard_map/reduce_scatter | solution.py:212
  683.3 200.7 %reduce-scatter.7.cloned.1.call-start = ((), (), s32[]{:S(2)}) async-start(), calls=%async_computation.7 | async-start | bytes 15728640 | tf_op jit(solution)/shard_map/reduce_scatter | solution.py:181
  706.1 82.2 %copy-start.31 = (f32[3,512]{1,0:T(4,128)S(1)}, f32[3,512]{1,0:T(4,128)}, u32[]{:S(2)}) copy-start(f32[3,512]{1,0:T(4,128)} %copy-done.30) | copy-start | bytes 18436
  706.1 82.2 %copy-start.27 = (f32[3,512]{1,0:T(4,128)S(1)}, f32[3,512]{1,0:T(4,128)}, u32[]{:S(2)}) copy-start(f32[3,512]{1,0:T(4,128)} %copy-done.26) | copy-start | bytes 18436
  706.2 275.4 %all-gather.11.cloned.1.call-start = ((), (), s32[]{:S(2)}) async-start(), calls=%async_computation.10 | async-start | bytes 15728640 | tf_op jit(solution)/shard_map/all_gather | solution.py:220
  788.4 95.6 %copy-start.42 = (f32[1024]{0:T(1024)S(1)}, f32[1024]{0:T(1024)}, u32[]{:S(2)}) copy-start(f32[1024]{0:T(1024)} %param.37) | copy-start | bytes 12292
  788.4 95.6 %copy-start.44 = (f32[3]{0:T(128)S(1)}, f32[3]{0:T(128)}, u32[]{:S(2)}) copy-start(f32[3]{0:T(128)} %copy-done.43) | copy-start | bytes 40
  899.2 902.9 %all-reduce.5.cloned.1.call-start = ((), (), s32[]{:S(2)}) async-start(), calls=%async_computation.12 | async-start | bytes 12582912 | tf_op jit(solution)/shard_map/psum | solution.py:268
  918.9 62.7 %copy-start.19 = (bf16[256,1024]{1,0:T(8,128)(2,1)S(1)}, bf16[256,1024]{1,0:T(8,128)(2,1)}, u32[]{:S(2)}) copy-start(bf16[256,1024]{1,0:T(8,128)(2,1)} %param.32) | copy-start | bytes 1572868
  1028.9 17.5 copy-start.6
  1068.4 17.5 copy-start.6
  1108.0 17.5 copy-start.6
  1147.5 17.5 copy-start.6
  1587.3 315.7 %reduce-scatter.11.cloned.1.call-start = ((), (), s32[]{:S(2)}) async-start(), calls=%async_computation.11 | async-start | bytes 15728640 | tf_op jit(solution)/shard_map/reduce_scatter | solution.py:261
  1812.1 90.8 %copy-start.22 = (f32[3,512]{1,0:T(4,128)S(1)}, f32[3,512]{1,0:T(4,128)}, u32[]{:S(2)}) copy-start(f32[3,512]{1,0:T(4,128)} %copy-done.21) | copy-start | bytes 18436
  1812.1 90.8 %copy-start.34 = (f32[1024]{0:T(1024)S(1)}, f32[1024]{0:T(1024)}, u32[]{:S(2)}) copy-start(f32[1024]{0:T(1024)} %param.38) | copy-start | bytes 12292
  1818.0 89.3 %copy-start.29 = (f32[3,512]{1,0:T(4,128)S(1)}, f32[3,512]{1,0:T(4,128)}, u32[]{:S(2)}) copy-start(f32[3,512]{1,0:T(4,128)} %copy-done.28) | copy-start | bytes 18436
  1818.0 89.4 %copy-start.25 = (f32[3,512]{1,0:T(4,128)S(1)}, f32[3,512]{1,0:T(4,128)}, u32[]{:S(2)}) copy-start(f32[3,512]{1,0:T(4,128)} %copy-done.24) | copy-start | bytes 18436
  1821.7 91.2 %copy-start.35 = (f32[1024]{0:T(1024)S(1)}, f32[1024]{0:T(1024)}, u32[]{:S(2)}) copy-start(f32[1024]{0:T(1024)} %get-tuple-element.318) | copy-start | bytes 12292
  1821.7 91.2 %copy-start.36 = (f32[1024]{0:T(1024)S(1)}, f32[1024]{0:T(1024)}, u32[]{:S(2)}) copy-start(f32[1024]{0:T(1024)} %get-tuple-element.314) | copy-start | bytes 12292
  1821.7 91.2 %copy-start.37 = (f32[1024]{0:T(1024)S(1)}, f32[1024]{0:T(1024)}, u32[]{:S(2)}) copy-start(f32[1024]{0:T(1024)} %get-tuple-element.396) | copy-start | bytes 12292
  1821.7 91.2 %copy-start.38 = (f32[1024]{0:T(1024)S(1)}, f32[1024]{0:T(1024)}, u32[]{:S(2)}) copy-start(f32[1024]{0:T(1024)} %get-tuple-element.411) | copy-start | bytes 12292
  (97 other events, 587.0 us)
Sparse Core Ops, SparseCore 0:
  16.5 84.7 all-gather.4
  347.2 99.0 reduce-scatter.4
  456.9 82.0 all-gather.6
  540.5 82.0 all-gather.8
  683.4 99.0 reduce-scatter.8
  785.0 99.0 reduce-scatter.6
  899.4 82.1 all-gather.10
  1587.4 214.7 all-reduce.4
  1804.9 97.9 reduce-scatter.10
where the time goes:
time: 1990 us; the launch traced here: 1970 us
  waiting for transfers between devices  715 us (36%)
  matrix products  649 us (33%)
  other arithmetic  334 us (17%)
  local copies, waits for them, and re-layouts  196 us (10%)
  blocking collectives  62.6 us (3%)
    psum x1, waiting for transfers between devices, shards(): lax.psum(query_key_value_gradient.astype(jnp.bfloat16), 'dp')  168 us
    convert_element_type x12, other arithmetic, one_block(): grad_low = grad_scores.astype(jnp.bfloat16)  127 us
    dot_general x12, matrix products, one_block(): jnp.einsum('qhd,khd->hqk', grad_block, values, preferred_element_type=jnp...  113 us
    reduce_scatter x1, waiting for transfers between devices, shards(): lax.psum_scatter(attn_part.astype(jnp.bfloat16), 'tensor', scatter_dimens...  99.1 us
    reduce_scatter x1, waiting for transfers between devices, shards(): lax.psum_scatter(perceptron_portion.astype(jnp.bfloat16), 'tensor', scatt...  88.3 us
    all_gather x1, waiting for transfers between devices, shards(): normalized_every = lax.all_gather(normed, 'tensor', axis=1, tiled=True)  84.7 us
    dot_general x12, matrix products, one_block(): jnp.einsum('hqk,khd->qhd', grad_low, key_rows, preferred_element_type=jnp...  82.8 us
    dot_general x24, matrix products, one_block(): jnp.einsum('qhd,khd->hqk', query_block, key_rows, preferred_element_type=...  82.5 us
  transfers between devices with their start and end apart: 9, of which 8 were waited for; matrix products, arithmetic and copies ran while one was open for 11% of the time, Pallas kernels for 0%

commit v1 on v0

--- a/solution.py
+++ b/solution.py
@@ -5,6 +5,26 @@
 
 HD = 64
 epsilon = 1e-05
+
+
+def _reach_tasks(frame, on_dim):
+    carry_out = list(frame.shape[1:])
+    carry_out[on_dim] *= frame.shape[0]
+    a_next = jnp.moveaxis(frame, 0, on_dim).reshape(carry_out)
+    return a_next
+
+
+def forms_press(slab_in, a_name):
+    tmp, out_arr = (jax.lax.axis_size(a_name), jax.lax.axis_index(a_name))
+    u_next, d_next = (slab_in[None], 1)
+    while d_next < tmp:
+        next_value = jax.lax.ppermute(u_next, a_name, [(no, no ^ d_next) for no in range(tmp)])
+        block_last = out_arr & d_next == 0
+        u_next = jnp.concatenate(
+            [jnp.where(block_last, u_next, next_value), jnp.where(block_last, next_value, u_next)]
+        )
+        d_next *= 2
+    return u_next
 
 
 def norm_rows(source, norm_gain, norm_shift):
@@ -160,7 +180,7 @@
     normed_mlp = norm_rows(residual, mlp_gain, mlp_shift).astype(half_type)
     cot_scaled = cotangent.astype(number_format) * own_scale[:, None, None]
     cot_low = cot_scaled.astype(half_type)
-    normalized_perceptron_every = lax.all_gather(normed_mlp, "tensor", axis=1, tiled=True)
+    normalized_perceptron_every = _reach_tasks(forms_press(normed_mlp, "tensor"), 1)
     hidden_pre = (
         jnp.einsum(
             "jzb,bu->jzu",

time: 1990 us -> 2140 us (1.075)
  waiting for transfers between devices: 715 us -> 843 us
    ppermute x0 -> x2, waiting for transfers between devices: none -> 203 us  [forms_press(): jax.lax.ppermute(u_next, a_name, [(no, no ^ d_next) for no in range(tmp)])]
    all_gather x1 -> x0, waiting for transfers between devices: 73.9 us -> none  [shards(): lax.all_gather(normed_mlp, 'tensor', axis=1, tiled=True)]
  transfers between devices with their start and end apart: 9 -> 10, of which waited for: 8 -> 9; matrix products, arithmetic and copies ran while one was open for 11% -> 11% of each run, Pallas kernels for 0% -> 0%
where the time goes in v1:
time: 2140 us; the launch traced here: 2130 us
  waiting for transfers between devices  843 us (39%)
  matrix products  646 us (30%)
  other arithmetic  348 us (16%)
  local copies, waits for them, and re-layouts  204 us (10%)
  blocking collectives  62.6 us (3%)
    ppermute x2, waiting for transfers between devices, forms_press(): jax.lax.ppermute(u_next, a_name, [(no, no ^ d_next) for no in range(tmp)])  203 us
    psum x1, waiting for transfers between devices, shards(): lax.psum(query_key_value_gradient.astype(jnp.bfloat16), 'dp')  168 us
    convert_element_type x12, other arithmetic, one_block(): grad_low = grad_scores.astype(jnp.bfloat16)  127 us
    dot_general x12, matrix products, one_block(): jnp.einsum('qhd,khd->hqk', grad_block, values, preferred_element_type=jnp...  110 us
    reduce_scatter x1, waiting for transfers between devices, shards(): lax.psum_scatter(attn_part.astype(jnp.bfloat16), 'tensor', scatter_dimens...  99.2 us
    reduce_scatter x1, waiting for transfers between devices, shards(): lax.psum_scatter(perceptron_portion.astype(jnp.bfloat16), 'tensor', scatt...  88.3 us
    all_gather x1, waiting for transfers between devices, shards(): normalized_every = lax.all_gather(normed, 'tensor', axis=1, tiled=True)  84.7 us
    dot_general x12, matrix products, one_block(): jnp.einsum('hqk,khd->qhd', grad_low, key_rows, preferred_element_type=jnp...  82.8 us
  transfers between devices with their start and end apart: 10, of which 9 were waited for; matrix products, arithmetic and copies ran while one was open for 11% of the time, Pallas kernels for 0%

profile of v1, /device:TPU:0, one launch (start us, length us, event | category | flops | bytes accessed | tf_op | source)
XLA Modules:
  0.0 2130.4 jit_solution(7073875466351213030)
XLA Ops:
  16.7 84.7 %all-gather.4.cloned.1.call-done = bf16[3,2048,1024]{2,1,0:T(8,128)(2,1)} async-done(((bf16[3,512,1024]{2,1,0:T(8,128)(2,1)}), bf16[3,2048,1024]{2,1,0:T(8,128)(2,1)}) %all-gather.4.cloned.1.call-update) | async-done | bytes 12582928 | tf_op jit(solution)/shard_map/all_gather | solution.py:156
  101.4 17.1 fusion.58
  123.4 11.4 fusion.103
  144.1 202.5 %while.54 = (s32[]{:T(128)}, bf16[3,2048,4,64]{1,3,2,0:T(8,128)(2,1)}, f32[3,4,4,512]{3,2,1,0:T(4,128)}, bf16[3,2048,4,64]{1,3,2,0:T(8,128)(2,1)}, bf16[3,2048,4...) while((s32[]{:T(128)}, ...), condition=%wide.region_7.8_spmd, body=%wide.region_2.7_spmd.sunk | while | flops 1111619584 | bytes 74055984 | solution.py:168
  162.2 47.4 %while.57 = (s32[]{:T(128)}, bf16[4,512,4,64]{1,3,2,0:T(8,128)(2,1)}, f32[4,4,512]{2,1,0:T(4,128)S(1)}, bf16[4,512,4,64]{1,3,2,0:T(8,128)(2,1)}, bf16[2048,4,64]...) while((s32[]{:T(128)}, bf16[4,512,4,64]{1,3,2,0:T(8,128)(2,1)}, ...), condition=%wide.region_6.6_spmd, body=%wide.region_3.5_spmd.sunk | while | flops 1111619584 | bytes 57213052 | solution.py:66
  226.4 47.4 %while.57 = (s32[]{:T(128)}, bf16[4,512,4,64]{1,3,2,0:T(8,128)(2,1)}, f32[4,4,512]{2,1,0:T(4,128)S(1)}, bf16[4,512,4,64]{1,3,2,0:T(8,128)(2,1)}, bf16[2048,4,64]...) while((s32[]{:T(128)}, bf16[4,512,4,64]{1,3,2,0:T(8,128)(2,1)}, ...), condition=%wide.region_6.6_spmd, body=%wide.region_3.5_spmd.sunk | while | flops 1111619584 | bytes 57213052 | solution.py:66
  290.6 47.4 %while.57 = (s32[]{:T(128)}, bf16[4,512,4,64]{1,3,2,0:T(8,128)(2,1)}, f32[4,4,512]{2,1,0:T(4,128)S(1)}, bf16[4,512,4,64]{1,3,2,0:T(8,128)(2,1)}, bf16[2048,4,64]...) while((s32[]{:T(128)}, bf16[4,512,4,64]{1,3,2,0:T(8,128)(2,1)}, ...), condition=%wide.region_6.6_spmd, body=%wide.region_3.5_spmd.sunk | while | flops 1111619584 | bytes 57213052 | solution.py:66
  356.9 99.2 %reduce-scatter.5.cloned.1.call-done = bf16[3,512,1024]{2,1,0:T(8,128)(2,1)} async-done(((bf16[3,2048,1024]{2,1,0:T(8,128)(2,1)}), bf16[3,512,1024]{2,1,0:T(8,128)(2,1)}) %reduce-scatter.5.cloned.1.call-update) | async-done | bytes 3145744 | tf_op jit(solution)/shard_map/reduce_scatter | solution.py:176
  488.5 196.6 %collective-permute-done.1 = bf16[2,3,512,1024]{3,2,1,0:T(8,128)(2,1)} collective-permute-done((bf16[2,3,512,1024]{3,2,1,0:T(8,128)(2,1)}, bf16[2,3,512,1024]{3,2,1,0:T(8,128)(2,1)}, u32[]{:S(2)}, u32[]{:S(2)}) %collective-permute-start.1) | collective-permute-done | bytes 6291488 | tf_op jit(solution)/shard_map/ppermute | solution.py:21
  697.0 29.6 %fusion.72 = (u8[2048,1024]{1,0:T(8,128)(4,1)}, u8[2048,1024]{1,0:T(8,128)(4,1)}, f32[3,2048,1024]{2,1,0:T(8,128)}) fusion(f32[1024]{0:T(1024)S(1)} %copy-done.49, bf16[3,2048,1024]{2,1,0:T(8,128)(2,1)} %bitcast.217, bf16[1024,1024]{1,0:T(8,128)(2,1)S(1)} %copy-done), kind=kOutput, calls=%fused_computation.132 | convolution fusion | flops 12968787968 | bytes 44044288 | tf_op jit(solution)/shard_map/jzb,bu->jzu/dot_general | solution.py:185
  726.5 61.6 %multiply_convert_fusion.1 = (bf16[3,2048,1024]{2,1,0:T(8,128)(2,1)}, f32[3,2048,1024]{2,1,0:T(8,128)}) fusion(f32[3,2048,1024]{2,1,0:T(8,128)} %get-tuple-element.416, f32[1024]{0:T(1024)S(1)} %copy-done.49, u8[2048,1024]{1,0:T(8,128)(4,1)} %get-tuple-element.313, u8[2048,1024]{1,0:T(8,128)(4,1)} %get-tuple-element.312), kind=kLoop, calls=%fused_computation.67 | loop fusion | flops 446693376 | bytes 67112960 | tf_op jit(solution)/shard_map/convert_element_type | solution.py:194
  788.1 32.8 %fusion.104 = (bf16[1024]{0:T(1024)(128)(2,1)}, bf16[3,2048,1024]{2,1,0:T(8,128)(2,1)}) fusion(f32[3,2048,1024]{2,1,0:T(8,128)} %get-tuple-element.399, bf16[3,2048,1024]{2,1,0:T(8,128)(2,1)} %all-gather.6.cloned.1.call-done, bf16[1024,1024]{1,0:T(8,128)(2,1)} %param.36, f32[3,2048,1024]{2,1,0:T(8,128)} %get-tuple-element.416, f32[1024]{0:T(1024)S(1)} %copy-done.49), kind=kOutput, calls=%fused_computation.199 | convolution fusion | flops 12985564160 | bytes 77600768 | tf_op jit(solution)/shard_map/eph,wh->epw/dot_general | solution.py:206
  821.0 20.3 convolution_convert_fusion
  842.8 21.2 convolution_convert_fusion.1
  864.8 75.7 %reduce-scatter.9.cloned.1.call-done = bf16[3,512,1024]{2,1,0:T(8,128)(2,1)} async-done(((bf16[3,2048,1024]{2,1,0:T(8,128)(2,1)}), bf16[3,512,1024]{2,1,0:T(8,128)(2,1)}) %reduce-scatter.9.cloned.1.call-update) | async-done | bytes 3145744 | tf_op jit(solution)/shard_map/reduce_scatter | solution.py:232
  953.7 88.3 %reduce-scatter.7.cloned.1.call-done = bf16[3,512,1024]{2,1,0:T(8,128)(2,1)} async-done(((bf16[3,2048,1024]{2,1,0:T(8,128)(2,1)}), bf16[3,512,1024]{2,1,0:T(8,128)(2,1)}) %reduce-scatter.7.cloned.1.call-update) | async-done | bytes 3145744 | tf_op jit(solution)/shard_map/reduce_scatter | solution.py:201
  1057.4 19.3 bitcast_convert_fusion.2
  1076.7 18.9 bitcast_convert_fusion.1
  1095.6 44.0 %all-gather.8.cloned.1.call-done = bf16[3,2048,1024]{2,1,0:T(8,128)(2,1)} async-done(((bf16[3,512,1024]{2,1,0:T(8,128)(2,1)}), bf16[3,2048,1024]{2,1,0:T(8,128)(2,1)}) %all-gather.8.cloned.1.call-update) | async-done | bytes 12582928 | tf_op jit(solution)/shard_map/all_gather | solution.py:240
  1139.6 14.3 convolution_convert_fusion.3
  1153.8 552.1 %while.56 = (s32[]{:T(128)}, bf16[3,2048,4,64]{1,3,2,0:T(8,128)(2,1)}, bf16[3,2048,4,64]{1,3,2,0:T(8,128)(2,1)}, bf16[3,2048,4,64]{1,3,2,0:T(8,128)(2,1)}, bf16[...) while((s32[]{:T(128)}, ...), condition=%wide.region_22.23_spmd, body=%wide.region_18.22_spmd.sunk | while | flops 2737436672 | bytes 246014544 | solution.py:255
  1169.0 157.6 %while.58 = (s32[]{:T(128)}, f32[2048,4,64]{0,2,1:T(8,128)}, f32[2048,4,64]{0,2,1:T(8,128)}, bf16[4,512,4,64]{1,3,2,0:T(8,128)(2,1)}, bf16[4,512,4,64]{1,3,2,0:T...) while((s32[]{:T(128)}, f32[2048,4,64]{0,2,1:T(8,128)}, ...), condition=%wide.region_21.21_spmd.clone, body=%wide.region_19.20_spmd.clone.sunk | while | flops 2737436672 | bytes 206102832 | solution.py:110
  1186.9 10.6 multiply_convert_fusion.4
  1265.7 10.6 multiply_convert_fusion.4
  1352.9 157.6 %while.58 = (s32[]{:T(128)}, f32[2048,4,64]{0,2,1:T(8,128)}, f32[2048,4,64]{0,2,1:T(8,128)}, bf16[4,512,4,64]{1,3,2,0:T(8,128)(2,1)}, bf16[4,512,4,64]{1,3,2,0:T...) while((s32[]{:T(128)}, f32[2048,4,64]{0,2,1:T(8,128)}, ...), condition=%wide.region_21.21_spmd.clone, body=%wide.region_19.20_spmd.clone.sunk | while | flops 2737436672 | bytes 206102832 | solution.py:110
  1536.8 157.6 %while.58 = (s32[]{:T(128)}, f32[2048,4,64]{0,2,1:T(8,128)}, f32[2048,4,64]{0,2,1:T(8,128)}, bf16[4,512,4,64]{1,3,2,0:T(8,128)(2,1)}, bf16[4,512,4,64]{1,3,2,0:T...) while((s32[]{:T(128)}, f32[2048,4,64]{0,2,1:T(8,128)}, ...), condition=%wide.region_21.21_spmd.clone, body=%wide.region_19.20_spmd.clone.sunk | while | flops 2737436672 | bytes 206102832 | solution.py:110
  1729.8 13.9 fusion.87
  1745.1 15.4 bitcast_convert_fusion
  1765.5 22.8 %all-reduce.1 = (bf16[2,256]{1,0:T(2,128)(2,1)S(1)}, bf16[1024]{0:T(1024)(128)(2,1)S(1)}) all-reduce(bf16[2,256]{1,0:T(2,128)(2,1)S(1)} %pad_maximum_fusion.8, bf16[1024]{0:T(1024)(128)(2,1)S(1)} %copy-done.53), channel_id=1, replica_groups=mesh['dp'=8,'tensor'=4] {'dp'}, use_global_device_ids=true, to_apply=%region_29.30 | all-reduce | flops 1536 | bytes 6144 | tf_op jit(solution)/shard_map/psum | solution.py:289
  1790.8 167.6 %all-reduce.5.cloned.1.call-done = (bf16[3,1024,256]{1,2,0:T(8,128)(2,1)}, bf16[256,1024]{1,0:T(8,128)(2,1)}, bf16[1024,1024]{1,0:T(8,128)(2,1)}, bf16[1024,1024]{1,0:T(8,128)(2,1)}) async-done(((bf16[3,1024,256]{1,2,0:T(8,128)(2,1)}, bf16[256,1024]{1,0:T(8,128)(2,1)}, bf16[1024,1024]{1,0:T(8,128)(2,1)}, bf16[1024,1024]{1,0:T(8,128)(2,1)}), (bf16[3,1024,256]{1,2,0:T(8,128)(2,1)}, ...) | async-done | bytes 6291472 | tf_op jit(solution)/shard_map/psum | solution.py:288
  1977.9 81.3 %reduce-scatter.11.cloned.1.call-done = bf16[3,512,1024]{2,1,0:T(8,128)(2,1)} async-done(((bf16[3,2048,1024]{2,1,0:T(8,128)(2,1)}), bf16[3,512,1024]{2,1,0:T(8,128)(2,1)}) %reduce-scatter.11.cloned.1.call-update) | async-done | bytes 3145744 | tf_op jit(solution)/shard_map/reduce_scatter | solution.py:281
  2069.2 39.8 %all-reduce = (f32[1024]{0:T(1024)S(1)}, f32[1024]{0:T(1024)S(1)}, f32[1024]{0:T(1024)S(1)}, f32[1024]{0:T(1024)S(1)}, f32[1024]{0:T(1024)S(1)}, /*index=5*/f32[1024]{0:T(1024)S(1)}) all-reduce(f32[1024]{0:T(1024)S(1)} %copy-done.43, f32[1024]{0:T(1024)S(1)} %copy-done.44, ...), channel_id=1, replica_groups=mesh['dp'=8,'tensor'=4] {'dp','tensor'}, use_global_device_ids=true, to_apply=%region_32.33 | all-reduce | flops 6144 | bytes 49152 | tf_op jit(solution)/shard_map/psum | solution.py:295
  (556 shorter events, 907.1 us)
Async XLA Ops:
  7.2 689.8 %copy-start = (bf16[1024,1024]{1,0:T(8,128)(2,1)S(1)}, bf16[1024,1024]{1,0:T(8,128)(2,1)}, u32[]{:S(2)}) copy-start(bf16[1024,1024]{1,0:T(8,128)(2,1)} %param.34) | copy-start | bytes 6291460
  7.2 94.1 %all-gather.4.cloned.1.call-start = ((), (), s32[]{:S(2)}) async-start(), calls=%async_computation.4 | async-start | bytes 15728640 | tf_op jit(solution)/shard_map/all_gather | solution.py:156
  16.4 439.6 %reduce-scatter.5.cloned.1.call-start = ((), (), s32[]{:S(2)}) async-start(), calls=%async_computation.5 | async-start | bytes 15728640 | tf_op jit(solution)/shard_map/reduce_scatter | solution.py:176
  356.8 99.3 %copy-start.27 = (f32[1024]{0:T(1024)S(1)}, f32[1024]{0:T(1024)}, u32[]{:S(2)}) copy-start(f32[1024]{0:T(1024)} %param.33) | copy-start | bytes 12292
  356.8 106.2 %copy-start.37 = (f32[1024]{0:T(1024)S(1)}, f32[1024]{0:T(1024)}, u32[]{:S(2)}) copy-start(f32[1024]{0:T(1024)} %param.40) | copy-start | bytes 12292
  356.8 106.2 %copy-start.47 = (f32[1024]{0:T(1024)S(1)}, f32[1024]{0:T(1024)}, u32[]{:S(2)}) copy-start(f32[1024]{0:T(1024)} %param.41) | copy-start | bytes 12292
  356.8 431.3 %all-gather.6.cloned.1.call-start = ((), (), s32[]{:S(2)}) async-start(), calls=%async_computation.7 | async-start | bytes 15728640 | tf_op jit(solution)/shard_map/all_gather | solution.py:205
  466.0 6.0 collective-permute-start
  479.8 205.3 %collective-permute-start.1 = (bf16[2,3,512,1024]{3,2,1,0:T(8,128)(2,1)}, bf16[2,3,512,1024]{3,2,1,0:T(8,128)(2,1)}, u32[]{:S(2)}, u32[]{:S(2)}) collective-permute-start(bf16[2,3,512,1024]{3,2,1,0:T(8,128)(2,1)} %pad_maximum_fusion.1), channel_id=1, source_target_pairs={{0,2},{1,3},{2,0},{3,1},{4,6},{5,7},{6,4},{7,5},{8,10},{9,11},{10,... | collective-permute-start | bytes 18874376 | tf_op jit(solution)/shard_map/ppermute | solution.py:21
  480.3 210.2 %copy-start.45 = (s32[24]{0:T(128)}, s32[24]{0:T(128)S(1)}, u32[]{:S(2)}) copy-start(s32[24]{0:T(128)S(1)} %reshape.223) | copy-start | bytes 292
  488.5 452.0 %reduce-scatter.9.cloned.1.call-start = ((), (), s32[]{:S(2)}) async-start(), calls=%async_computation.8 | async-start | bytes 15728640 | tf_op jit(solution)/shard_map/reduce_scatter | solution.py:232
  841.3 200.8 %reduce-scatter.7.cloned.1.call-start = ((), (), s32[]{:S(2)}) async-start(), calls=%async_computation.6 | async-start | bytes 15728640 | tf_op jit(solution)/shard_map/reduce_scatter | solution.py:201
  864.1 76.4 %copy-start.26 = (f32[3,512]{1,0:T(4,128)S(1)}, f32[3,512]{1,0:T(4,128)}, u32[]{:S(2)}) copy-start(f32[3,512]{1,0:T(4,128)} %copy-done.25) | copy-start | bytes 18436
  864.1 76.4 %copy-start.28 = (f32[1024]{0:T(1024)S(1)}, f32[1024]{0:T(1024)}, u32[]{:S(2)}) copy-start(f32[1024]{0:T(1024)} %param.33) | copy-start | bytes 12292
  864.1 76.4 %copy-start.38 = (f32[1024]{0:T(1024)S(1)}, f32[1024]{0:T(1024)}, u32[]{:S(2)}) copy-start(f32[1024]{0:T(1024)} %param.40) | copy-start | bytes 12292
  864.1 82.3 %copy-start.36 = (f32[3,512]{1,0:T(4,128)S(1)}, f32[3,512]{1,0:T(4,128)}, u32[]{:S(2)}) copy-start(f32[3,512]{1,0:T(4,128)} %copy-done.35) | copy-start | bytes 18436
  864.1 82.3 %copy-start.32 = (f32[3,512]{1,0:T(4,128)S(1)}, f32[3,512]{1,0:T(4,128)}, u32[]{:S(2)}) copy-start(f32[3,512]{1,0:T(4,128)} %copy-done.31) | copy-start | bytes 18436
  864.1 275.5 %all-gather.8.cloned.1.call-start = ((), (), s32[]{:S(2)}) async-start(), calls=%async_computation.9 | async-start | bytes 15728640 | tf_op jit(solution)/shard_map/all_gather | solution.py:240
  946.4 95.7 %copy-start.50 = (f32[1024]{0:T(1024)S(1)}, f32[1024]{0:T(1024)}, u32[]{:S(2)}) copy-start(f32[1024]{0:T(1024)} %param.37) | copy-start | bytes 12292
  946.4 95.7 %copy-start.52 = (f32[3]{0:T(128)S(1)}, f32[3]{0:T(128)}, u32[]{:S(2)}) copy-start(f32[3]{0:T(128)} %copy-done.51) | copy-start | bytes 40
  1057.3 901.1 %all-reduce.5.cloned.1.call-start = ((), (), s32[]{:S(2)}) async-start(), calls=%async_computation.11 | async-start | bytes 12582912 | tf_op jit(solution)/shard_map/psum | solution.py:288
  1076.7 62.9 %copy-start.21 = (bf16[256,1024]{1,0:T(8,128)(2,1)S(1)}, bf16[256,1024]{1,0:T(8,128)(2,1)}, u32[]{:S(2)}) copy-start(bf16[256,1024]{1,0:T(8,128)(2,1)} %param.32) | copy-start | bytes 1572868
  1186.9 17.5 copy-start.6
  1743.7 315.5 %reduce-scatter.11.cloned.1.call-start = ((), (), s32[]{:S(2)}) async-start(), calls=%async_computation.10 | async-start | bytes 15728640 | tf_op jit(solution)/shard_map/reduce_scatter | solution.py:281
  1968.3 90.9 %copy-start.24 = (f32[3,512]{1,0:T(4,128)S(1)}, f32[3,512]{1,0:T(4,128)}, u32[]{:S(2)}) copy-start(f32[3,512]{1,0:T(4,128)} %copy-done.23) | copy-start | bytes 18436
  1968.3 90.9 %copy-start.40 = (f32[1024]{0:T(1024)S(1)}, f32[1024]{0:T(1024)}, u32[]{:S(2)}) copy-start(f32[1024]{0:T(1024)} %param.38) | copy-start | bytes 12292
  1974.2 89.3 %copy-start.34 = (f32[3,512]{1,0:T(4,128)S(1)}, f32[3,512]{1,0:T(4,128)}, u32[]{:S(2)}) copy-start(f32[3,512]{1,0:T(4,128)} %copy-done.33) | copy-start | bytes 18436
  1974.2 89.4 %copy-start.30 = (f32[3,512]{1,0:T(4,128)S(1)}, f32[3,512]{1,0:T(4,128)}, u32[]{:S(2)}) copy-start(f32[3,512]{1,0:T(4,128)} %copy-done.29) | copy-start | bytes 18436
  1977.9 91.2 %copy-start.41 = (f32[1024]{0:T(1024)S(1)}, f32[1024]{0:T(1024)}, u32[]{:S(2)}) copy-start(f32[1024]{0:T(1024)} %get-tuple-element.318) | copy-start | bytes 12292
  1977.9 91.2 %copy-start.42 = (f32[1024]{0:T(1024)S(1)}, f32[1024]{0:T(1024)}, u32[]{:S(2)}) copy-start(f32[1024]{0:T(1024)} %get-tuple-element.314) | copy-start | bytes 12292
  1977.9 91.2 %copy-start.43 = (f32[1024]{0:T(1024)S(1)}, f32[1024]{0:T(1024)}, u32[]{:S(2)}) copy-start(f32[1024]{0:T(1024)} %get-tuple-element.396) | copy-start | bytes 12292
  1977.9 91.2 %copy-start.44 = (f32[1024]{0:T(1024)S(1)}, f32[1024]{0:T(1024)}, u32[]{:S(2)}) copy-start(f32[1024]{0:T(1024)} %get-tuple-element.415) | copy-start | bytes 12292
  (106 other events, 664.1 us)
Sparse Core Ops, SparseCore 0:
  16.5 84.7 all-gather.3
  356.9 99.0 reduce-scatter.4
  488.6 150.7 all-gather.5
  841.4 99.0 reduce-scatter.8
  942.9 99.0 reduce-scatter.6
  1057.4 82.1 all-gather.7
  1743.8 214.5 all-reduce.4
  1961.1 97.9 reduce-scatter.10
